TPU v7x, 32 devices: a whole 2x2x4 slice. The times are simulated.
32 devices in a mesh: dp: 8 (over z, y), tensor: 4 (over x, core).
Axes of the slice: x: 2, y: 2, z: 4, core: 2. Of those that a mesh axis runs over, the one named last changes fastest.
Arguments:
- tokens: bfloat16 [512, 1536], P('dp'), may hold values from -6 to 6
- norm_gain: float32 [1536], replicated, may hold values from 0.1 to 1.9
- w_query: bfloat16 [1536, 1024], P(None, 'tensor'), may hold values from -0.15625 to 0.15625
- w_keyval: bfloat16 [1536, 256], replicated, may hold values from -0.15625 to 0.15625
- w_out: bfloat16 [1024, 1536], P('tensor'), may hold values from -0.5 to 0.5
- kv_pool: bfloat16 [4096, 128, 256], P(('dp', 'tensor')), may hold values from -256 to 256
- page_table: int32 [512, 8], P('dp', 'tensor'), may hold values from 0 to 127, as said below
- positions: int32 [512], P('dp'), may hold values from 0 to 8191
- assignment: int32 [512], P('dp'), may hold values from 0 to 511, as said below
Outputs:
- attn_out: bfloat16 [512, 1536], P('dp')
Inputs may be any that keep to these rules, and one draw needn't show every extreme that they name: `assignment`: the serving slot is the serving device's dp index times 64 plus a local slot; each serving slot is taken by exactly one request; the 64 requests of one device go to 8 distinct devices, exactly 8 to each. `page_table`: on each device the entries form a permutation of 0 to 127.
All inputs are finite; a program needn't handle non-finite values.
Results may differ from a plain program's by a relative error of at most 0.03.
Values may be sent and summed in bfloat16 or wider, within the bound.
A program may use at most 64 MiB of HBM per device.

v0:
```python
import jax
import jax.numpy as jnp
from jax import lax
from jax.sharding import PartitionSpec as P

masked_score = -1e30
norm_eps = 1e-06
rotary_base = 10000.0


def combined_all(array, axis, join):
    gathered = jax.tree.map(
        lambda a, kind: lax.all_gather(a.astype(kind), axis),
        array,
        (jnp.bfloat16, jnp.bfloat16, jnp.bfloat16),
    )

    def take(source):
        return jax.tree.map(
            lambda a, own: lax.dynamic_index_in_dim(a, source, 0, False).astype(own.dtype),
            gathered,
            array,
        )

    return lax.fori_loop(
        1, lax.axis_size(axis), lambda source, state: join(state, take(source)), take(0)
    )


def as_sent(array):

    def short(part):
        return part.astype(jnp.bfloat16) if part.dtype == jnp.float32 else part

    return jax.tree.map(short, array)


def rotate(values, where, width):
    half = width // 2
    freqs = rotary_base ** (-jnp.arange(half, dtype=jnp.float32) * 2.0 / width)
    angles = where.astype(jnp.float32)[..., None] * freqs
    cosine = jnp.cos(angles)
    sine = jnp.sin(angles)
    first = values[..., :half]
    second = values[..., half:]
    return jnp.concatenate(
        [first * cosine - second * sine, first * sine + second * cosine], axis=-1
    )


def combine_stats(first, second):
    peak = jnp.maximum(first[0], second[0])
    first_scale = jnp.exp(first[0] - peak)
    second_scale = jnp.exp(second[0] - peak)
    total = first[1] * first_scale + second[1] * second_scale
    summed = first[2] * first_scale[..., None] + second[2] * second_scale[..., None]
    return (peak, total, summed)


def local(tokens, norm_gain, w_query, w_keyval, w_out, kv_pool, page_table, positions, assignment):
    head_width = w_keyval.shape[1] // 2
    row_count = tokens.shape[0]
    group_size = lax.axis_size("tensor")
    data_size = lax.axis_size("dp")
    local_heads = w_query.shape[1] // head_width
    all_heads = local_heads * group_size
    capacity = max(2, row_count // data_size)
    slots_all = data_size * capacity
    scale = head_width ** (-0.5)
    here = lax.axis_index("tensor")
    floats = tokens.astype(jnp.float32)
    normed = (
        floats * lax.rsqrt(jnp.mean(floats * floats, axis=-1, keepdims=True) + norm_eps) * norm_gain
    ).astype(jnp.bfloat16)
    query = jnp.dot(normed, w_query, preferred_element_type=jnp.float32).reshape(
        row_count, local_heads, head_width
    )
    query = rotate(query, positions[:, None], head_width).astype(jnp.bfloat16)
    key_value = jnp.dot(normed, w_keyval, preferred_element_type=jnp.float32)
    new_key = rotate(key_value[:, :head_width], positions, head_width).astype(jnp.bfloat16)
    new_value = key_value[:, head_width:].astype(jnp.bfloat16)
    target = assignment // row_count
    local_slot = assignment % row_count
    hits = (target[:, None] == jnp.arange(data_size, dtype=jnp.int32)[None, :]).astype(jnp.int32)
    order_in = jnp.sum(jnp.cumsum(hits, axis=0) * hits, axis=1) - 1
    place = target * capacity + order_in

    def to_buffer(values):
        empty = jnp.zeros((slots_all,) + values.shape[1:], values.dtype)
        filled = empty.at[place].set(values)
        return filled.reshape((data_size, capacity) + values.shape[1:])

    def source_buffer(values):
        return values.reshape((slots_all,) + values.shape[2:])[place]

    tags = to_buffer(jnp.stack([positions, local_slot + 1], axis=1))
    tags = lax.all_to_all(tags, "dp", split_axis=0, concat_axis=0, tiled=True).reshape(slots_all, 2)
    served_slot = tags[:, 1] - 1
    scatter_slot = jnp.where(served_slot < 0, row_count, served_slot)
    gather_slot = jnp.maximum(served_slot, 0)

    def compact(values):
        empty = jnp.zeros((row_count,) + values.shape[1:], values.dtype)
        return empty.at[scatter_slot].set(values, mode="drop")

    def expand(values):
        return values[gather_slot].reshape((data_size, capacity) + values.shape[1:])

    current = compact(tags[:, 0])
    full_query = lax.all_gather(query, "tensor", axis=1, tiled=True)
    served_heads = lax.all_to_all(
        to_buffer(full_query), "dp", split_axis=0, concat_axis=0, tiled=True
    )
    served_heads = compact(served_heads.reshape(slots_all, all_heads, head_width))
    page_rows = page_table.shape[1]
    page_len = kv_pool.shape[1]
    window = page_rows * group_size * page_len
    page_entries = kv_pool[page_table].reshape(row_count, page_rows * page_len, 2 * head_width)
    scores = (
        jnp.einsum(
            "vto,vio->vti",
            served_heads,
            page_entries[..., :head_width],
            preferred_element_type=jnp.float32,
        )
        * scale
    )
    cycle_slot = here * page_rows * page_len + jnp.arange(page_rows * page_len, dtype=jnp.int32)
    offset = jnp.mod(cycle_slot[None, :] - current[:, None], window)
    valid = ((offset != 0) & (current[:, None] - window + offset >= 0))[:, None, :]
    peak = jnp.max(jnp.where(valid, scores, masked_score), axis=2)
    weight_tensors = jnp.where(valid, jnp.exp(scores - peak[..., None]), 0.0)
    total = jnp.sum(weight_tensors, axis=2)
    summed = jnp.einsum(
        "rbi,ril->rbl",
        weight_tensors.astype(jnp.bfloat16),
        page_entries[..., head_width:],
        preferred_element_type=jnp.float32,
    )
    merged = combined_all((peak, total, summed), "tensor", combine_stats)
    returned = (
        lax.all_to_all(as_sent(expand(merged[0])), "dp", split_axis=0, concat_axis=0, tiled=True),
        lax.all_to_all(as_sent(expand(merged[1])), "dp", split_axis=0, concat_axis=0, tiled=True),
        lax.all_to_all(as_sent(expand(merged[2])), "dp", split_axis=0, concat_axis=0, tiled=True),
    )
    own_stats = tuple(
        (
            lax.dynamic_slice_in_dim(source_buffer(member), here * local_heads, local_heads, 1)
            for member in returned
        )
    )
    cache_peak, cache_total, cache_summed = own_stats
    self_score = (
        jnp.einsum("rhd,rd->rh", query, new_key, preferred_element_type=jnp.float32) * scale
    )
    overall = jnp.maximum(cache_peak, self_score)
    keep = jnp.exp(cache_peak - overall)
    fresh = jnp.exp(self_score - overall)
    full_total = cache_total * keep + fresh
    fresh_low = fresh.astype(jnp.bfloat16).astype(jnp.float32)
    full_summed = (
        cache_summed * keep[..., None]
        + fresh_low[..., None] * new_value.astype(jnp.float32)[:, None, :]
    )
    attended = (
        (full_summed / full_total[..., None])
        .astype(jnp.bfloat16)
        .reshape(row_count, local_heads * head_width)
    )
    partial_out = jnp.dot(attended, w_out, preferred_element_type=jnp.float32)
    return lax.psum(partial_out.astype(jnp.bfloat16), "tensor")


def solution(mesh):
    return jax.shard_map(
        local,
        mesh=mesh,
        in_specs=(
            P("dp", None),
            P(),
            P(None, "tensor"),
            P(),
            P("tensor", None),
            P(("dp", "tensor"), None, None),
            P("dp", "tensor"),
            P("dp"),
            P("dp"),
        ),
        out_specs=P("dp", None),
        check_vma=False,
    )
```

profile of v0, /device:TPU:0, one launch (start us, length us, event | category | flops | bytes accessed | tf_op | source)
XLA Modules:
  0.0 160.3 jit_solution(12733547716529152877)
XLA Ops:
  6.5 0.7 fusion.43
  7.3 0.7 pad_add_fusion
  7.9 0.1 copy.66
  8.1 0.1 reduce_window_sum.11
  8.2 0.2 select_reduce_fusion.1
  8.4 0.8 scatter_custom_fusion
  9.2 0.7 copy.68
  9.9 7.3 %all-to-all-start = ((s32[8,8,2]{1,2,0:T(2,128)}), s32[8,8,2]{1,2,0:T(2,128)S(1)}, u32[]{:S(2)}, u32[]{:S(2)}) async-start(s32[8,8,2]{1,2,0:T(2,128)} %copy.68), calls=%async_computation | async-start | bytes 16384 | tf_op jit(solution)/shard_map/all_to_all | solution.py:97
  17.2 0.7 convert_element_type.152
  17.8 1.1 fusion.15
  18.9 0.7 compare_select_fusion
  19.6 0.1 copy.73
  19.7 0.1 reshape.222
  19.9 1.6 fusion.25
  21.4 1.6 fusion.27
  23.0 0.1 fusion.50
  23.2 0.2 subtract_convert_fusion.1
  23.5 0.1 pad_maximum_fusion
  23.6 0.2 fusion.32
  23.8 5.4 %all_gather.17 = bf16[64,8,128]{2,0,1:T(8,128)(2,1)S(1)} all-gather(bf16[64,2,128]{2,0,1:T(8,128)(2,1)S(1)} %pad_maximum_fusion), channel_id=1, replica_groups=mesh['dp'=8,'tensor'=4] {'tensor'}, dimensions={1}, use_global_device_ids=true | all-gather | bytes 163840 | tf_op jit(solution)/shard_map/all_gather | solution.py:110
  29.2 0.1 copy.72
  29.3 0.7 broadcast.188.clone
  30.0 6.9 %scatter_fusion = bf16[64,8,128]{2,1,0:T(8,128)(2,1)} fusion(bf16[64,8,128]{2,1,0:T(8,128)(2,1)} %broadcast.188.clone, s32[64]{0:T(128)S(1)} %compare_select_fusion.3, bf16[64,8,128]{2,1,0:T(8,128)(2,1)S(1)} %copy.72), kind=kCustom, calls=%fused_computation.9 | custom fusion | bytes 393472 | tf_op jit(solution)/shard_map/scatter | solution.py:90
  36.9 10.0 %gather_fusion = bf16[128,128,256]{2,1,0:T(8,128)(2,1)} fusion(bf16[128,128,256]{2,1,0:T(8,128)(2,1)} %param.16, s32[1024]{0:T(1024)S(1)} %pad_clamp_fusion.2), kind=kCustom, calls=%fused_computation | custom fusion | bytes 16777728 | tf_op jit(solution)/shard_map/gather | solution.py:118
  46.8 6.0 %all-to-all-start.1 = ((bf16[8,8,8,128]{3,2,1,0:T(8,128)(2,1)}), bf16[8,8,8,128]{3,2,1,0:T(8,128)(2,1)S(1)}, u32[]{:S(2)}, u32[]{:S(2)}) async-start(bf16[8,8,8,128]{3,2,1,0:T(8,128)(2,1)} %bitcast.9), calls=%async_computation.1 | async-start | bytes 262144 | tf_op jit(solution)/shard_map/all_to_all | solution.py:111
  52.9 0.8 scatter_custom_fusion.1
  53.7 0.1 fusion.24
  53.8 6.5 %all-to-all-done.1 = bf16[8,8,8,128]{3,2,1,0:T(8,128)(2,1)S(1)} async-done(((bf16[8,8,8,128]{3,2,1,0:T(8,128)(2,1)}), bf16[8,8,8,128]{3,2,1,0:T(8,128)(2,1)S(1)}, u32[]{:S(2)}, u32[]{:S(2)}) %all-to-all-start.1) | async-done | bytes 131104 | tf_op jit(solution)/shard_map/all_to_all | solution.py:111
  60.3 2.5 %scatter_fusion.1 = bf16[64,8,128]{2,1,0:T(8,128)(2,1)S(1)} fusion(bf16[64,8,128]{2,1,0:T(8,128)(2,1)S(1)} %broadcast.188, s32[64]{0:T(128)S(1)} %get-tuple-element.216, bf16[64,8,128]{2,1,0:T(8,128)(2,1)S(1)} %bitcast.88), kind=kCustom, calls=%fused_computation.10 | custom fusion | bytes 393472 | tf_op jit(solution)/shard_map/scatter | solution.py:104
  62.8 3.5 %select_reduce_fusion = (f32[64,8]{1,0:T(8,128)S(1)}, f32[64,8,256]{2,1,0:T(8,128)S(1)}) fusion(pred[64,256]{1,0:T(8,128)(4,1)S(1)} %fusion.24, bf16[64,8,128]{2,1,0:T(8,128)(2,1)S(1)} %scatter_fusion.1, bf16[64,256,256]{2,1,0:T(8,128)(2,1)} %bitcast.82), kind=kOutput, calls=%fused_computation.27 | convolution fusion | flops 33947136 | bytes 4868096 | tf_op jit(solution)/shard_map/vto,vio->vti/dot_general | solution.py:120
  66.3 2.9 %fusion.10 = bf16[64,8,128]{2,1,0:T(8,128)(2,1)S(1)} fusion(bf16[64,256,256]{2,1,0:T(8,128)(2,1)} %bitcast.83, f32[64,8,256]{2,1,0:T(8,128)S(1)} %get-tuple-element.221, f32[64,8]{1,0:T(8,128)S(1)} %get-tuple-element.220, pred[64,256]{1,0:T(8,128)(4,1)S(1)} %fusion.24), kind=kOutput, calls=%fused_computation.25 | convolution fusion | flops 34013184 | bytes 4868096 | tf_op jit(solution)/shard_map/rbi,ril->rbl/dot_general | solution.py:134
  69.2 0.3 fusion.14
  69.6 5.2 %all-gather.4 = bf16[4,64,8]{1,2,0:T(8,128)(2,1)S(1)} all-gather(bf16[1,64,8]{1,2,0:T(8,128)(2,1)S(1)} %copy.75), channel_id=3, replica_groups=mesh['dp'=8,'tensor'=4] {'tensor'}, dimensions={0}, use_global_device_ids=true | all-gather | bytes 5120 | tf_op jit(solution)/shard_map/all_gather | solution.py:13
  74.8 5.1 %all-gather.3 = bf16[4,64,8]{1,2,0:T(8,128)(2,1)S(1)} all-gather(bf16[1,64,8]{1,2,0:T(8,128)(2,1)S(1)} %copy.74), channel_id=2, replica_groups=mesh['dp'=8,'tensor'=4] {'tensor'}, dimensions={0}, use_global_device_ids=true | all-gather | bytes 5120 | tf_op jit(solution)/shard_map/all_gather | solution.py:13
  79.9 7.2 %all-gather.2 = bf16[256,8,128]{2,1,0:T(8,128)(2,1)S(1)} all-gather(bf16[64,8,128]{2,1,0:T(8,128)(2,1)S(1)} %fusion.10), channel_id=4, replica_groups=mesh['dp'=8,'tensor'=4] {'tensor'}, dimensions={0}, use_global_device_ids=true | all-gather | bytes 655360 | tf_op jit(solution)/shard_map/all_gather | solution.py:13
  87.2 1.5 while.19
  87.2 0.1 copy.114
  87.4 0.3 fusion.58
  87.7 0.1 copy.114
  87.9 0.3 fusion.58
  88.2 0.1 copy.114
  88.4 0.3 fusion.58
  88.7 0.1 copy.76
  88.8 1.2 gather_fusion.3
  90.0 3.3 %all-to-all-start.3 = ((bf16[8,8,8]{2,1,0:T(8,128)(2,1)}), bf16[8,8,8]{2,1,0:T(8,128)(2,1)S(1)}, u32[]{:S(2)}, u32[]{:S(2)}) async-start(bf16[8,8,8]{2,1,0:T(8,128)(2,1)} %bitcast.65), calls=%async_computation.3 | async-start | bytes 32768 | tf_op jit(solution)/shard_map/all_to_all | solution.py:142
  93.4 0.1 copy.80
  93.5 1.2 gather_fusion.5
  94.7 5.2 %all-to-all-done.3 = bf16[8,8,8]{2,1,0:T(8,128)(2,1)S(1)} async-done(((bf16[8,8,8]{2,1,0:T(8,128)(2,1)}), bf16[8,8,8]{2,1,0:T(8,128)(2,1)S(1)}, u32[]{:S(2)}, u32[]{:S(2)}) %all-to-all-start.3) | async-done | bytes 1056 | tf_op jit(solution)/shard_map/all_to_all | solution.py:142
  99.9 3.3 %all-to-all-start.4 = ((bf16[8,8,8]{2,1,0:T(8,128)(2,1)}), bf16[8,8,8]{2,1,0:T(8,128)(2,1)S(1)}, u32[]{:S(2)}, u32[]{:S(2)}) async-start(bf16[8,8,8]{2,1,0:T(8,128)(2,1)} %bitcast.64), calls=%async_computation.4 | async-start | bytes 32768 | tf_op jit(solution)/shard_map/all_to_all | solution.py:143
  103.3 1.3 gather_fusion.1
  104.6 0.6 gather_fusion.4
  105.2 4.5 %all-to-all-done.4 = bf16[8,8,8]{2,1,0:T(8,128)(2,1)S(1)} async-done(((bf16[8,8,8]{2,1,0:T(8,128)(2,1)}), bf16[8,8,8]{2,1,0:T(8,128)(2,1)S(1)}, u32[]{:S(2)}, u32[]{:S(2)}) %all-to-all-start.4) | async-done | bytes 1056 | tf_op jit(solution)/shard_map/all_to_all | solution.py:143
  109.7 3.4 %all-to-all-start.2 = ((bf16[8,8,8,128]{3,2,1,0:T(8,128)(2,1)}), bf16[8,8,8,128]{3,2,1,0:T(8,128)(2,1)S(1)}, u32[]{:S(2)}, u32[]{:S(2)}) async-start(bf16[8,8,8,128]{3,2,1,0:T(8,128)(2,1)} %bitcast.18), calls=%async_computation.2 | async-start | bytes 262144 | tf_op jit(solution)/shard_map/all_to_all | solution.py:144
  113.2 0.6 gather_fusion.6
  114.0 0.1 copy.90
  114.1 0.1 copy.82
  114.2 0.1 copy.78
  114.3 0.1 copy.79
  114.4 6.0 %all-to-all-done.2 = bf16[8,8,8,128]{3,2,1,0:T(8,128)(2,1)S(1)} async-done(((bf16[8,8,8,128]{3,2,1,0:T(8,128)(2,1)}), bf16[8,8,8,128]{3,2,1,0:T(8,128)(2,1)S(1)}, u32[]{:S(2)}, u32[]{:S(2)}) %all-to-all-start.2) | async-done | bytes 131104 | tf_op jit(solution)/shard_map/all_to_all | solution.py:144
  120.4 0.6 gather_fusion.2
  121.0 0.3 fusion.23
  121.3 0.9 convolution_convert_fusion
  122.3 29.6 %all-reduce.2.cloned.1.call-done = bf16[64,1536]{1,0:T(8,128)(2,1)} async-done(((bf16[64,1536]{1,0:T(8,128)(2,1)}), bf16[64,1536]{1,0:T(8,128)(2,1)}) %all-reduce.2.cloned.1.call-update) | async-done | bytes 196624 | tf_op jit(solution)/shard_map/psum | solution.py:171
  151.8 1.6 %copy.131 = bf16[64,1536]{1,0:T(8,128)(2,1)} copy(bf16[64,1536]{1,0:T(8,128)(2,1)} %all-reduce.2.cloned.1.call-done) | data formatting | bytes 393216
  (38 shorter events, 1.2 us)
Async XLA Ops:
  6.5 114.8 %copy-start = (bf16[256,1536]{1,0:T(8,128)(2,1)S(1)}, bf16[256,1536]{1,0:T(8,128)(2,1)}, u32[]{:S(2)}) copy-start(bf16[256,1536]{1,0:T(8,128)(2,1)} %param.15) | copy-start | bytes 2359300
  9.9 37.0 %all-to-all-start = ((s32[8,8,2]{1,2,0:T(2,128)}), s32[8,8,2]{1,2,0:T(2,128)S(1)}, u32[]{:S(2)}, u32[]{:S(2)}) async-start(s32[8,8,2]{1,2,0:T(2,128)} %copy.68), calls=%async_computation | async-start | bytes 16384 | tf_op jit(solution)/shard_map/all_to_all | solution.py:97
  46.8 13.5 %all-to-all-start.1 = ((bf16[8,8,8,128]{3,2,1,0:T(8,128)(2,1)}), bf16[8,8,8,128]{3,2,1,0:T(8,128)(2,1)S(1)}, u32[]{:S(2)}, u32[]{:S(2)}) async-start(bf16[8,8,8,128]{3,2,1,0:T(8,128)(2,1)} %bitcast.9), calls=%async_computation.1 | async-start | bytes 262144 | tf_op jit(solution)/shard_map/all_to_all | solution.py:111
  90.0 9.9 %all-to-all-start.3 = ((bf16[8,8,8]{2,1,0:T(8,128)(2,1)}), bf16[8,8,8]{2,1,0:T(8,128)(2,1)S(1)}, u32[]{:S(2)}, u32[]{:S(2)}) async-start(bf16[8,8,8]{2,1,0:T(8,128)(2,1)} %bitcast.65), calls=%async_computation.3 | async-start | bytes 32768 | tf_op jit(solution)/shard_map/all_to_all | solution.py:142
  99.9 9.9 %all-to-all-start.4 = ((bf16[8,8,8]{2,1,0:T(8,128)(2,1)}), bf16[8,8,8]{2,1,0:T(8,128)(2,1)S(1)}, u32[]{:S(2)}, u32[]{:S(2)}) async-start(bf16[8,8,8]{2,1,0:T(8,128)(2,1)} %bitcast.64), calls=%async_computation.4 | async-start | bytes 32768 | tf_op jit(solution)/shard_map/all_to_all | solution.py:143
  109.7 10.7 %all-to-all-start.2 = ((bf16[8,8,8,128]{3,2,1,0:T(8,128)(2,1)}), bf16[8,8,8,128]{3,2,1,0:T(8,128)(2,1)S(1)}, u32[]{:S(2)}, u32[]{:S(2)}) async-start(bf16[8,8,8,128]{3,2,1,0:T(8,128)(2,1)} %bitcast.18), calls=%async_computation.2 | async-start | bytes 262144 | tf_op jit(solution)/shard_map/all_to_all | solution.py:144
  113.1 38.7 %all-reduce.2.cloned.1.call-start = ((), (), s32[]{:S(2)}) async-start(), calls=%async_computation.5 | async-start | bytes 393216 | tf_op jit(solution)/shard_map/psum | solution.py:171
Sparse Core Ops, SparseCore 0:
  122.4 29.3 all-reduce.1
where the time goes:
time: 161 us; the launch traced here: 160 us
  waiting for transfers between devices  51.7 us (32%)
  local copies, waits for them, and re-layouts  31.7 us (20%)
  starting transfers between devices  23.4 us (15%)
  blocking collectives  23 us (14%)
  between operations  13.6 us (8%)
  matrix products  10.6 us (7%)
  other arithmetic  6.19 us (4%)
    psum x1, waiting for transfers between devices, local(): return lax.psum(partial_out.astype(jnp.bfloat16), 'tensor')  29.6 us
    all_gather x3, blocking collectives, combined_all(): lax.all_gather(a.astype(kind), axis)  17.6 us
    gather x1, local copies, waits for them, and re-layouts, local(): kv_pool[page_table].reshape(row_count, page_rows * page_len, 2 * head_width)  9.96 us
    scatter x2, local copies, waits for them, and re-layouts, to_buffer(): filled = empty.at[place].set(values)  7.66 us
    all_to_all x1, starting transfers between devices, local(): lax.all_to_all(tags, 'dp', split_axis=0, concat_axis=0, tiled=True)  7.28 us
    all_to_all x1, waiting for transfers between devices, local(): lax.all_to_all(to_buffer(full_query), 'dp', split_axis=0, concat_axis=0,...  6.47 us
    all_to_all x1, waiting for transfers between devices, local(): lax.all_to_all(as_sent(expand(merged[2])), 'dp', split_axis=0, concat_axi...  6.02 us
    all_to_all x1, starting transfers between devices, local(): lax.all_to_all(to_buffer(full_query), 'dp', split_axis=0, concat_axis=0,...  6 us
  transfers between devices with their start and end apart: 6, of which 5 were waited for; matrix products, arithmetic and copies ran while one was open for 19% of the time, Pallas kernels for 0%

commit v1 on v0

--- a/solution.py
+++ b/solution.py
@@ -58,6 +58,10 @@
 
 
 def local(tokens, norm_gain, w_query, w_keyval, w_out, kv_pool, page_table, positions, assignment):
+
+    def runs_post(base_x, along_axis="tensor"):
+        return jnp.sum(lax.all_gather(base_x, along_axis), 0)
+
     head_width = w_keyval.shape[1] // 2
     row_count = tokens.shape[0]
     group_size = lax.axis_size("tensor")
@@ -168,7 +172,7 @@
         .reshape(row_count, local_heads * head_width)
     )
     partial_out = jnp.dot(attended, w_out, preferred_element_type=jnp.float32)
-    return lax.psum(partial_out.astype(jnp.bfloat16), "tensor")
+    return runs_post(partial_out.astype(jnp.bfloat16))
 
 
 def solution(mesh):

time: 161 us -> 125 us (0.78)
  waiting for transfers between devices: 51.7 us -> 22.2 us
  between operations: 13.6 us -> 0.25 us
  blocking collectives: 23 us -> 31.6 us
  local copies, waits for them, and re-layouts: 31.7 us -> 30 us
    psum x1 -> x0, waiting for transfers between devices: 29.6 us -> none  [local(): return lax.psum(partial_out.astype(jnp.bfloat16), 'tensor')]
    all_gather x0 -> x1, blocking collectives: none -> 8.6 us  [runs_post(): return jnp.sum(lax.all_gather(base_x, along_axis), 0)]
    unnamed x7 -> x6, local copies, waits for them, and re-layouts: 1.94 us -> 0.32 us
  transfers between devices with their start and end apart: 6 -> 5, of which waited for: 5 -> 4; matrix products, arithmetic and copies ran while one was open for 19% -> 24% of each run, Pallas kernels for 0% -> 0%
where the time goes in v1:
time: 125 us; the launch traced here: 124 us
  blocking collectives  31.6 us (25%)
  local copies, waits for them, and re-layouts  30 us (24%)
  starting transfers between devices  23.3 us (19%)
  waiting for transfers between devices  22.2 us (18%)
  matrix products  9.94 us (8%)
  other arithmetic  7 us (6%)
    all_gather x3, blocking collectives, combined_all(): lax.all_gather(a.astype(kind), axis)  17.6 us
    gather x1, local copies, waits for them, and re-layouts, local(): kv_pool[page_table].reshape(row_count, page_rows * page_len, 2 * head_width)  9.96 us
    all_gather x1, blocking collectives, runs_post(): return jnp.sum(lax.all_gather(base_x, along_axis), 0)  8.6 us
    scatter x2, local copies, waits for them, and re-layouts, to_buffer(): filled = empty.at[place].set(values)  7.66 us
    all_to_all x1, starting transfers between devices, local(): lax.all_to_all(tags, 'dp', split_axis=0, concat_axis=0, tiled=True)  7.28 us
    all_to_all x1, waiting for transfers between devices, local(): lax.all_to_all(to_buffer(full_query), 'dp', split_axis=0, concat_axis=0,...  6.47 us
    all_to_all x1, waiting for transfers between devices, local(): lax.all_to_all(as_sent(expand(merged[2])), 'dp', split_axis=0, concat_axi...  6.06 us
    all_to_all x1, starting transfers between devices, local(): lax.all_to_all(to_buffer(full_query), 'dp', split_axis=0, concat_axis=0,...  6 us
  transfers between devices with their start and end apart: 5, of which 4 were waited for; matrix products, arithmetic and copies ran while one was open for 24% of the time, Pallas kernels for 0%

profile of v1, /device:TPU:0, one launch (start us, length us, event | category | flops | bytes accessed | tf_op | source)
XLA Modules:
  0.0 124.4 jit_solution(3898094773547497958)
XLA Ops:
  0.0 0.7 fusion.43
  0.7 0.7 pad_add_fusion
  1.4 0.1 copy.66
  1.6 0.1 reduce_window_sum.11
  1.7 0.2 select_reduce_fusion.1
  1.9 0.8 scatter_custom_fusion
  2.6 0.7 copy.68
  3.3 7.3 %all-to-all-start = ((s32[8,8,2]{1,2,0:T(2,128)}), s32[8,8,2]{1,2,0:T(2,128)S(1)}, u32[]{:S(2)}, u32[]{:S(2)}) async-start(s32[8,8,2]{1,2,0:T(2,128)} %copy.68), calls=%async_computation | async-start | bytes 16384 | tf_op jit(solution)/shard_map/all_to_all | solution.py:101
  10.6 0.7 convert_element_type.154
  11.3 1.1 fusion.15
  12.4 0.7 compare_select_fusion
  13.1 0.1 copy.73
  13.2 0.1 reshape.222
  13.3 1.6 %fusion.25 = f32[64,256]{1,0:T(8,128)S(1)} fusion(bf16[1536,256]{1,0:T(8,128)(2,1)} %param.14, bf16[64,1536]{1,0:T(8,128)(2,1)} %param.11, f32[1536]{0:T(1024)} %param.12, f32[64]{0:T(128)S(1)} %add_rsqrt_fusion), kind=kOutput, calls=%fused_computation.51 | convolution fusion | flops 50724864 | bytes 1054976 | tf_op jit(solution)/shard_map/dot_general | solution.py:83
  14.9 1.6 %fusion.27 = f32[64,256]{1,0:T(8,128)S(1)} fusion(bf16[1536,256]{1,0:T(8,128)(2,1)} %param.13, bf16[64,1536]{1,0:T(8,128)(2,1)} %param.11, f32[1536]{0:T(1024)} %param.12, f32[64]{0:T(128)S(1)} %add_rsqrt_fusion), kind=kOutput, calls=%fused_computation.52 | convolution fusion | flops 50724864 | bytes 1054976 | tf_op jit(solution)/shard_map/dot_general | solution.py:79
  16.5 0.1 fusion.50
  16.6 0.2 subtract_convert_fusion.1
  16.9 0.1 pad_maximum_fusion
  17.0 0.2 fusion.32
  17.2 5.4 %all_gather.23 = bf16[64,8,128]{2,0,1:T(8,128)(2,1)S(1)} all-gather(bf16[64,2,128]{2,0,1:T(8,128)(2,1)S(1)} %pad_maximum_fusion), channel_id=1, replica_groups=mesh['dp'=8,'tensor'=4] {'tensor'}, dimensions={1}, use_global_device_ids=true | all-gather | bytes 163840 | tf_op jit(solution)/shard_map/all_gather | solution.py:114
  22.7 0.1 copy.72
  22.7 0.7 broadcast.188.clone
  23.4 6.9 %scatter_fusion = bf16[64,8,128]{2,1,0:T(8,128)(2,1)} fusion(bf16[64,8,128]{2,1,0:T(8,128)(2,1)} %broadcast.188.clone, s32[64]{0:T(128)S(1)} %compare_select_fusion.3, bf16[64,8,128]{2,1,0:T(8,128)(2,1)S(1)} %copy.72), kind=kCustom, calls=%fused_computation.9 | custom fusion | bytes 393472 | tf_op jit(solution)/shard_map/scatter | solution.py:94
  30.3 10.0 %gather_fusion = bf16[128,128,256]{2,1,0:T(8,128)(2,1)} fusion(bf16[128,128,256]{2,1,0:T(8,128)(2,1)} %param.16, s32[1024]{0:T(1024)S(1)} %pad_clamp_fusion.2), kind=kCustom, calls=%fused_computation | custom fusion | bytes 16777728 | tf_op jit(solution)/shard_map/gather | solution.py:122
  40.3 6.0 %all-to-all-start.1 = ((bf16[8,8,8,128]{3,2,1,0:T(8,128)(2,1)}), bf16[8,8,8,128]{3,2,1,0:T(8,128)(2,1)S(1)}, u32[]{:S(2)}, u32[]{:S(2)}) async-start(bf16[8,8,8,128]{3,2,1,0:T(8,128)(2,1)} %bitcast.9), calls=%async_computation.1 | async-start | bytes 262144 | tf_op jit(solution)/shard_map/all_to_all | solution.py:115
  46.4 0.8 scatter_custom_fusion.1
  47.2 0.1 fusion.24
  47.3 6.5 %all-to-all-done.1 = bf16[8,8,8,128]{3,2,1,0:T(8,128)(2,1)S(1)} async-done(((bf16[8,8,8,128]{3,2,1,0:T(8,128)(2,1)}), bf16[8,8,8,128]{3,2,1,0:T(8,128)(2,1)S(1)}, u32[]{:S(2)}, u32[]{:S(2)}) %all-to-all-start.1) | async-done | bytes 131104 | tf_op jit(solution)/shard_map/all_to_all | solution.py:115
  53.8 2.5 %scatter_fusion.1 = bf16[64,8,128]{2,1,0:T(8,128)(2,1)S(1)} fusion(bf16[64,8,128]{2,1,0:T(8,128)(2,1)S(1)} %broadcast.188, s32[64]{0:T(128)S(1)} %get-tuple-element.216, bf16[64,8,128]{2,1,0:T(8,128)(2,1)S(1)} %bitcast.90), kind=kCustom, calls=%fused_computation.10 | custom fusion | bytes 393472 | tf_op jit(solution)/shard_map/scatter | solution.py:108
  56.3 3.5 %select_reduce_fusion = (f32[64,8]{1,0:T(8,128)S(1)}, f32[64,8,256]{2,1,0:T(8,128)S(1)}) fusion(pred[64,256]{1,0:T(8,128)(4,1)S(1)} %fusion.24, bf16[64,8,128]{2,1,0:T(8,128)(2,1)S(1)} %scatter_fusion.1, bf16[64,256,256]{2,1,0:T(8,128)(2,1)} %bitcast.83), kind=kOutput, calls=%fused_computation.27 | convolution fusion | flops 33947136 | bytes 4868096 | tf_op jit(solution)/shard_map/vto,vio->vti/dot_general | solution.py:124
  59.7 2.9 %fusion.10 = bf16[64,8,128]{2,1,0:T(8,128)(2,1)S(1)} fusion(bf16[64,256,256]{2,1,0:T(8,128)(2,1)} %bitcast.84, f32[64,8,256]{2,1,0:T(8,128)S(1)} %get-tuple-element.221, f32[64,8]{1,0:T(8,128)S(1)} %get-tuple-element.220, pred[64,256]{1,0:T(8,128)(4,1)S(1)} %fusion.24), kind=kOutput, calls=%fused_computation.25 | convolution fusion | flops 34013184 | bytes 4868096 | tf_op jit(solution)/shard_map/rbi,ril->rbl/dot_general | solution.py:138
  62.6 0.3 fusion.14
  63.1 5.2 %all-gather.5 = bf16[4,64,8]{1,2,0:T(8,128)(2,1)S(1)} all-gather(bf16[1,64,8]{1,2,0:T(8,128)(2,1)S(1)} %copy.75), channel_id=3, replica_groups=mesh['dp'=8,'tensor'=4] {'tensor'}, dimensions={0}, use_global_device_ids=true | all-gather | bytes 5120 | tf_op jit(solution)/shard_map/all_gather | solution.py:13
  68.3 5.1 %all-gather.4 = bf16[4,64,8]{1,2,0:T(8,128)(2,1)S(1)} all-gather(bf16[1,64,8]{1,2,0:T(8,128)(2,1)S(1)} %copy.74), channel_id=2, replica_groups=mesh['dp'=8,'tensor'=4] {'tensor'}, dimensions={0}, use_global_device_ids=true | all-gather | bytes 5120 | tf_op jit(solution)/shard_map/all_gather | solution.py:13
  73.4 7.2 %all-gather.2 = bf16[256,8,128]{2,1,0:T(8,128)(2,1)S(1)} all-gather(bf16[64,8,128]{2,1,0:T(8,128)(2,1)S(1)} %fusion.10), channel_id=4, replica_groups=mesh['dp'=8,'tensor'=4] {'tensor'}, dimensions={0}, use_global_device_ids=true | all-gather | bytes 655360 | tf_op jit(solution)/shard_map/all_gather | solution.py:13
  80.7 1.5 %while.19 = (s32[]{:T(128)}, f32[64,8]{0,1:T(8,128)S(1)}, f32[64,8]{0,1:T(8,128)S(1)}, f32[64,8,128]{2,1,0:T(8,128)S(1)}, bf16[4,64,8]{1,2,0:T(8,128)(2,1)S(1)},...) while((s32[]{:T(128)}, f32[64,8]{0,1:T(8,128)S(1)}, ...), condition=%wide.region_10.11_spmd, body=%wide.region_9.10_spmd.sunk | while | flops 266245 | bytes 682127 | solution.py:25
  80.7 0.1 copy.114
  80.9 0.3 fusion.58
  81.2 0.1 copy.114
  81.4 0.3 fusion.58
  81.7 0.1 copy.114
  81.9 0.3 fusion.58
  82.2 0.1 copy.76
  82.2 1.2 gather_fusion.3
  83.5 3.3 %all-to-all-start.3 = ((bf16[8,8,8]{2,1,0:T(8,128)(2,1)}), bf16[8,8,8]{2,1,0:T(8,128)(2,1)S(1)}, u32[]{:S(2)}, u32[]{:S(2)}) async-start(bf16[8,8,8]{2,1,0:T(8,128)(2,1)} %bitcast.66), calls=%async_computation.3 | async-start | bytes 32768 | tf_op jit(solution)/shard_map/all_to_all | solution.py:146
  86.8 0.1 copy.80
  86.9 1.2 gather_fusion.5
  88.2 5.2 %all-to-all-done.3 = bf16[8,8,8]{2,1,0:T(8,128)(2,1)S(1)} async-done(((bf16[8,8,8]{2,1,0:T(8,128)(2,1)}), bf16[8,8,8]{2,1,0:T(8,128)(2,1)S(1)}, u32[]{:S(2)}, u32[]{:S(2)}) %all-to-all-start.3) | async-done | bytes 1056 | tf_op jit(solution)/shard_map/all_to_all | solution.py:146
  93.3 3.3 %all-to-all-start.4 = ((bf16[8,8,8]{2,1,0:T(8,128)(2,1)}), bf16[8,8,8]{2,1,0:T(8,128)(2,1)S(1)}, u32[]{:S(2)}, u32[]{:S(2)}) async-start(bf16[8,8,8]{2,1,0:T(8,128)(2,1)} %bitcast.65), calls=%async_computation.4 | async-start | bytes 32768 | tf_op jit(solution)/shard_map/all_to_all | solution.py:147
  96.8 1.3 %gather_fusion.1 = bf16[64,8,128]{2,1,0:T(8,128)(2,1)} fusion(f32[64,8,128]{2,1,0:T(8,128)S(1)} %get-tuple-element.183, s32[1024]{0:T(1024)S(1)} %pad_clamp_fusion.1), kind=kCustom, calls=%fused_computation.1 | custom fusion | bytes 262400 | tf_op jit(solution)/shard_map/gather | solution.py:111
  98.1 0.6 gather_fusion.4
  98.7 4.5 %all-to-all-done.4 = bf16[8,8,8]{2,1,0:T(8,128)(2,1)S(1)} async-done(((bf16[8,8,8]{2,1,0:T(8,128)(2,1)}), bf16[8,8,8]{2,1,0:T(8,128)(2,1)S(1)}, u32[]{:S(2)}, u32[]{:S(2)}) %all-to-all-start.4) | async-done | bytes 1056 | tf_op jit(solution)/shard_map/all_to_all | solution.py:147
  103.2 3.4 %all-to-all-start.2 = ((bf16[8,8,8,128]{3,2,1,0:T(8,128)(2,1)}), bf16[8,8,8,128]{3,2,1,0:T(8,128)(2,1)S(1)}, u32[]{:S(2)}, u32[]{:S(2)}) async-start(bf16[8,8,8,128]{3,2,1,0:T(8,128)(2,1)} %bitcast.18), calls=%async_computation.2 | async-start | bytes 262144 | tf_op jit(solution)/shard_map/all_to_all | solution.py:148
  106.6 0.6 gather_fusion.6
  107.4 0.1 copy.90
  107.5 0.1 copy.82
  107.6 0.1 copy.78
  107.7 0.1 copy.79
  107.8 6.1 %all-to-all-done.2 = bf16[8,8,8,128]{3,2,1,0:T(8,128)(2,1)S(1)} async-done(((bf16[8,8,8,128]{3,2,1,0:T(8,128)(2,1)}), bf16[8,8,8,128]{3,2,1,0:T(8,128)(2,1)S(1)}, u32[]{:S(2)}, u32[]{:S(2)}) %all-to-all-start.2) | async-done | bytes 131104 | tf_op jit(solution)/shard_map/all_to_all | solution.py:148
  113.9 0.6 gather_fusion.2
  114.5 0.3 fusion.23
  114.8 0.3 convolution_convert_fusion
  115.0 8.6 %all-gather.3 = bf16[256,1536]{1,0:T(8,128)(2,1)S(1)} all-gather(bf16[64,1536]{1,0:T(8,128)(2,1)S(1)} %convolution_convert_fusion), channel_id=5, replica_groups=mesh['dp'=8,'tensor'=4] {'tensor'}, dimensions={0}, use_global_device_ids=true | all-gather | bytes 983040 | tf_op jit(solution)/shard_map/all_gather | solution.py:63
  123.6 0.8 reduce_sum.42
  (36 shorter events, 1.1 us)
Async XLA Ops:
  0.0 114.8 %copy-start = (bf16[256,1536]{1,0:T(8,128)(2,1)S(1)}, bf16[256,1536]{1,0:T(8,128)(2,1)}, u32[]{:S(2)}) copy-start(bf16[256,1536]{1,0:T(8,128)(2,1)} %param.15) | copy-start | bytes 2359300
  3.3 36.9 %all-to-all-start = ((s32[8,8,2]{1,2,0:T(2,128)}), s32[8,8,2]{1,2,0:T(2,128)S(1)}, u32[]{:S(2)}, u32[]{:S(2)}) async-start(s32[8,8,2]{1,2,0:T(2,128)} %copy.68), calls=%async_computation | async-start | bytes 16384 | tf_op jit(solution)/shard_map/all_to_all | solution.py:101
  40.3 13.5 %all-to-all-start.1 = ((bf16[8,8,8,128]{3,2,1,0:T(8,128)(2,1)}), bf16[8,8,8,128]{3,2,1,0:T(8,128)(2,1)S(1)}, u32[]{:S(2)}, u32[]{:S(2)}) async-start(bf16[8,8,8,128]{3,2,1,0:T(8,128)(2,1)} %bitcast.9), calls=%async_computation.1 | async-start | bytes 262144 | tf_op jit(solution)/shard_map/all_to_all | solution.py:115
  83.5 9.9 %all-to-all-start.3 = ((bf16[8,8,8]{2,1,0:T(8,128)(2,1)}), bf16[8,8,8]{2,1,0:T(8,128)(2,1)S(1)}, u32[]{:S(2)}, u32[]{:S(2)}) async-start(bf16[8,8,8]{2,1,0:T(8,128)(2,1)} %bitcast.66), calls=%async_computation.3 | async-start | bytes 32768 | tf_op jit(solution)/shard_map/all_to_all | solution.py:146
  93.3 9.9 %all-to-all-start.4 = ((bf16[8,8,8]{2,1,0:T(8,128)(2,1)}), bf16[8,8,8]{2,1,0:T(8,128)(2,1)S(1)}, u32[]{:S(2)}, u32[]{:S(2)}) async-start(bf16[8,8,8]{2,1,0:T(8,128)(2,1)} %bitcast.65), calls=%async_computation.4 | async-start | bytes 32768 | tf_op jit(solution)/shard_map/all_to_all | solution.py:147
  103.2 10.7 %all-to-all-start.2 = ((bf16[8,8,8,128]{3,2,1,0:T(8,128)(2,1)}), bf16[8,8,8,128]{3,2,1,0:T(8,128)(2,1)S(1)}, u32[]{:S(2)}, u32[]{:S(2)}) async-start(bf16[8,8,8,128]{3,2,1,0:T(8,128)(2,1)} %bitcast.18), calls=%async_computation.2 | async-start | bytes 262144 | tf_op jit(solution)/shard_map/all_to_all | solution.py:148
